TPU v7x, 32 devices: a whole 2x2x4 slice. The times are simulated.
32 devices in a mesh: dp: 8 (over z, y), tensor: 4 (over x, core).
Axes of the slice: x: 2, y: 2, z: 4, core: 2. Of those that a mesh axis runs over, the one named last changes fastest.
Arguments:
- inputs: bfloat16 [8192, 1024], P(('dp', 'tensor')), may hold values from -6 to 6
- doc_ids: int32 [8, 1024], P('dp'), may hold values from 0 to 1, as said below
- w_qkv: bfloat16 [3, 1024, 1024], P(None, None, 'tensor'), may hold values from -0.1875 to 0.1875
- w_out: bfloat16 [1024, 1024], P('tensor'), may hold values from -0.1875 to 0.1875
- w_up: bfloat16 [1024, 4096], P(None, 'tensor'), may hold values from -0.1875 to 0.1875
- w_down: bfloat16 [4096, 1024], P('tensor'), may hold values from -0.09375 to 0.09375
- norm_gain: float32 [4, 1024], replicated, may hold values from 0.25 to 1.75
- norm_bias: float32 [4, 1024], replicated, may hold values from -1.5 to 1.5
- out_grad: bfloat16 [8192, 1024], P(('dp', 'tensor')), may hold values from -6 to 6
Outputs:
- output: bfloat16 [8192, 1024], P(('dp', 'tensor'))
- grad_inputs: bfloat16 [8192, 1024], P(('dp', 'tensor'))
- grad_qkv: float32 [3, 1024, 1024], P(None, None, 'tensor')
- grad_wout: float32 [1024, 1024], P('tensor')
- grad_up: float32 [1024, 4096], P(None, 'tensor')
- grad_down: float32 [4096, 1024], P('tensor')
- grad_gain: float32 [4, 1024], replicated
- grad_bias: float32 [4, 1024], replicated
Inputs may be any that keep to these rules, and one draw needn't show every extreme that they name: `doc_ids`: in each group either every token is in document 0, or token i is in document i // 512; exactly half of the groups are of the first kind.
All inputs are finite; a program needn't handle non-finite values.
Results may differ from a plain program's by a relative error of at most 0.015.
Values may be sent and summed in bfloat16 or wider, within the bound.
No kernel may reach another device: no remote copies, remote signals or barrier semaphores. Data moves between devices by JAX's collectives and lax.ppermute only.
A program may use at most 128 MiB of HBM per device.

v0:
```python
import jax
import jax.numpy as jnp
from jax import lax
from jax.sharding import PartitionSpec as P

HEAD_DIM = 64
eps = 1e-05


def rope_tables(doc_row):
    length_all = doc_row.shape[0]
    places = jnp.arange(length_all, dtype=jnp.int32)
    earlier = jnp.concatenate([doc_row[:1], doc_row[:-1]])
    starting = jnp.logical_and(doc_row != earlier, places > 0)
    first_pos = lax.cummax(jnp.where(starting, places, 0), axis=0)
    place = (places - first_pos).astype(jnp.float32)
    half = HEAD_DIM // 2
    freqs = 10000.0 ** (-jnp.arange(half, dtype=jnp.float32) / half)
    angles = place[:, None] * freqs[None, :]
    return (jnp.cos(angles), jnp.sin(angles))


def rotate(values_in, cosine, sine_table):
    half = values_in.shape[-1] // 2
    first = values_in[..., :half]
    second = values_in[..., half:]
    cos_wide = cosine[:, None, :]
    sin_wide = sine_table[:, None, :]
    return jnp.concatenate(
        [first * cos_wide - second * sin_wide, second * cos_wide + first * sin_wide], axis=-1
    )


def rotate_back(grad_in, cosine, sine_table):
    half = grad_in.shape[-1] // 2
    first = grad_in[..., :half]
    second = grad_in[..., half:]
    cos_wide = cosine[:, None, :]
    sin_wide = sine_table[:, None, :]
    return jnp.concatenate(
        [first * cos_wide + second * sin_wide, second * cos_wide - first * sin_wide], axis=-1
    )


def block_mask(doc_row, offset, block_rows):
    places = jnp.arange(doc_row.shape[0], dtype=jnp.int32)
    query_pos = offset + jnp.arange(block_rows, dtype=jnp.int32)
    query_doc = lax.dynamic_slice_in_dim(doc_row, offset, block_rows, 0)
    return jnp.logical_and(
        places[None, :] <= query_pos[:, None], doc_row[None, :] == query_doc[:, None]
    )


def norm_forward(values_in, gain, bias):
    center = values_in - jnp.mean(values_in, axis=-1, keepdims=True)
    spread = jnp.mean(center * center, axis=-1, keepdims=True)
    scale_inv = lax.rsqrt(spread + eps)
    unit = center * scale_inv
    return (unit * gain + bias, unit, scale_inv)


def norm_backward(upstream, unit, scale_inv, gain):
    scaled = upstream * gain
    result = scale_inv * (
        scaled
        - jnp.mean(scaled, axis=-1, keepdims=True)
        - unit * jnp.mean(scaled * unit, axis=-1, keepdims=True)
    )
    return (result, jnp.sum(upstream * unit, axis=0), jnp.sum(upstream, axis=0))


def gelu_exact(values_in):
    return 0.5 * values_in * (1.0 + jax.scipy.special.erf(values_in * 0.7071067811865476))


def gelu_slope(values_in):
    return (
        0.5 * (1.0 + jax.scipy.special.erf(values_in * 0.7071067811865476))
        + values_in * jnp.exp(-0.5 * values_in * values_in) * 0.3989422804014327
    )


def gather_rows(values_in):
    return lax.all_gather(values_in, "tensor", axis=0, tiled=True)


def row_sums(term, own_rows):
    return lax.psum_scatter(
        term(jnp.int32(0), own_rows * lax.axis_size("tensor")),
        "tensor",
        scatter_dimension=0,
        tiled=True,
    )


def attention_forward(query_rot, key_rot, value_all, doc_row):
    length_all = query_rot.shape[0]
    block_rows = min(512, length_all)
    scaling = HEAD_DIM ** (-0.5)

    def attend(offset):
        query_block = lax.dynamic_slice_in_dim(query_rot, offset, block_rows, 0)
        scores = (
            jnp.einsum("qhd,khd->hqk", query_block, key_rot, preferred_element_type=jnp.float32)
            * scaling
        )
        scores = jnp.where(block_mask(doc_row, offset, block_rows)[None], scores, -1e30)
        row_max = jnp.max(scores, axis=-1, keepdims=True)
        exp_scores = jnp.exp(scores - row_max)
        row_total = jnp.sum(exp_scores, axis=-1, keepdims=True)
        weights = (exp_scores / row_total).astype(jnp.bfloat16)
        attended = jnp.einsum(
            "hqk,khd->qhd", weights, value_all, preferred_element_type=jnp.float32
        )
        return (attended.astype(jnp.bfloat16), (row_max + jnp.log(row_total))[..., 0])

    offsets = jnp.arange(length_all // block_rows, dtype=jnp.int32) * block_rows
    head_out, log_total = lax.map(attend, offsets)
    return (head_out.reshape(length_all, -1), log_total)


def attention_backward(query_rot, key_rot, value_all, doc_row, grad_heads, log_total):
    length_all = query_rot.shape[0]
    block_rows = min(512, length_all)
    scaling = HEAD_DIM ** (-0.5)

    def step_back(running, item):
        offset, total_block = item
        query_block = lax.dynamic_slice_in_dim(query_rot, offset, block_rows, 0)
        grad_block = lax.dynamic_slice_in_dim(grad_heads, offset, block_rows, 0)
        scores = (
            jnp.einsum("qhd,khd->hqk", query_block, key_rot, preferred_element_type=jnp.float32)
            * scaling
        )
        scores = jnp.where(block_mask(doc_row, offset, block_rows)[None], scores, -1e30)
        probs = jnp.exp(scores - total_block[..., None])
        grad_probs = jnp.einsum(
            "qhd,khd->hqk", grad_block, value_all, preferred_element_type=jnp.float32
        )
        delta = jnp.sum(probs * grad_probs, axis=-1, keepdims=True)
        grad_scores = (probs * (grad_probs - delta) * scaling).astype(jnp.bfloat16)
        grad_query = jnp.einsum(
            "hqk,khd->qhd", grad_scores, key_rot, preferred_element_type=jnp.float32
        )
        grad_key = running[0] + jnp.einsum(
            "hqk,qhd->khd", grad_scores, query_block, preferred_element_type=jnp.float32
        )
        grad_value = running[1] + jnp.einsum(
            "hqk,qhd->khd",
            probs.astype(jnp.bfloat16),
            grad_block,
            preferred_element_type=jnp.float32,
        )
        return ((grad_key, grad_value), grad_query)

    offsets = jnp.arange(length_all // block_rows, dtype=jnp.int32) * block_rows
    zeros_kv = jnp.zeros(key_rot.shape, jnp.float32)
    (grad_key, grad_value), grad_query = lax.scan(
        step_back, (zeros_kv, zeros_kv), (offsets, log_total)
    )
    return (grad_query.reshape(key_rot.shape), grad_key, grad_value)


def per_device(inputs, doc_ids, w_qkv, w_out, w_up, w_down, norm_gain, norm_bias, out_grad):
    own_rows = inputs.shape[0]
    doc_row = doc_ids[0]
    length_all = doc_row.shape[0]
    cosine, sine_table = rope_tables(doc_row)
    local_heads = w_qkv.shape[2] // HEAD_DIM
    shaped = (length_all, local_heads, HEAD_DIM)
    rows_f32 = inputs.astype(jnp.float32)
    normed, unit0, inv0 = norm_forward(rows_f32, norm_gain[0], norm_bias[0])
    gathered = gather_rows(normed.astype(jnp.bfloat16))
    projected = jnp.einsum("td,jde->jte", gathered, w_qkv, preferred_element_type=jnp.float32)
    query_rot = rotate(projected[0].reshape(shaped), cosine, sine_table).astype(jnp.bfloat16)
    key_rot = rotate(projected[1].reshape(shaped), cosine, sine_table).astype(jnp.bfloat16)
    value_all = projected[2].reshape(shaped).astype(jnp.bfloat16)
    head_flat, log_total = attention_forward(query_rot, key_rot, value_all, doc_row)

    def out_term(offset, amount):
        return jnp.dot(head_flat, w_out, preferred_element_type=jnp.float32)

    attended = row_sums(out_term, own_rows)
    attn_normed, unit1, inv1 = norm_forward(attended, norm_gain[1], norm_bias[1])
    middle = rows_f32 + attn_normed
    normed2, unit2, inv2 = norm_forward(middle, norm_gain[2], norm_bias[2])
    normed2_low = normed2.astype(jnp.bfloat16)
    gathered2 = gather_rows(normed2_low)
    hidden = jnp.dot(gathered2, w_up, preferred_element_type=jnp.float32)
    activated = gelu_exact(hidden).astype(jnp.bfloat16)

    def down_term(offset, amount):
        return jnp.dot(activated, w_down, preferred_element_type=jnp.float32)

    mixed = row_sums(down_term, own_rows)
    mixed_normed, unit3, inv3 = norm_forward(mixed, norm_gain[3], norm_bias[3])
    output = (middle + mixed_normed).astype(jnp.bfloat16)
    grad_out = out_grad.astype(jnp.float32)
    grad_mixed, gain3, bias3 = norm_backward(grad_out, unit3, inv3, norm_gain[3])
    grad_mixed_low = grad_mixed.astype(jnp.bfloat16)
    grad_mixed_all = gather_rows(grad_mixed_low)
    grad_down = jnp.einsum(
        "tf,td->fd", activated, grad_mixed_all, preferred_element_type=jnp.float32
    )
    grad_act = jnp.einsum("td,fd->tf", grad_mixed_all, w_down, preferred_element_type=jnp.float32)
    grad_hidden = (grad_act * gelu_slope(hidden)).astype(jnp.bfloat16)
    grad_up = jnp.einsum("td,tf->df", gathered2, grad_hidden, preferred_element_type=jnp.float32)

    def up_term(offset, amount):
        return jnp.einsum("tf,df->td", grad_hidden, w_up, preferred_element_type=jnp.float32)

    grad_normed2 = row_sums(up_term, own_rows)
    back2, gain2, bias2 = norm_backward(grad_normed2, unit2, inv2, norm_gain[2])
    grad_middle = grad_out + back2
    grad_attended, gain1, bias1 = norm_backward(grad_middle, unit1, inv1, norm_gain[1])
    grad_attended_all = gather_rows(grad_attended.astype(jnp.bfloat16))
    grad_wout = jnp.einsum(
        "te,td->ed", head_flat, grad_attended_all, preferred_element_type=jnp.float32
    )
    grad_heads = (
        jnp.einsum("td,ed->te", grad_attended_all, w_out, preferred_element_type=jnp.float32)
        .astype(jnp.bfloat16)
        .reshape(shaped)
    )
    grad_query, grad_key, grad_value = attention_backward(
        query_rot, key_rot, value_all, doc_row, grad_heads, log_total
    )
    flat_width = local_heads * HEAD_DIM
    grad_proj = jnp.stack(
        [
            rotate_back(grad_query, cosine, sine_table).reshape(length_all, flat_width),
            rotate_back(grad_key, cosine, sine_table).reshape(length_all, flat_width),
            grad_value.reshape(length_all, flat_width),
        ],
        axis=0,
    ).astype(jnp.bfloat16)
    grad_qkv = jnp.einsum("td,jte->jde", gathered, grad_proj, preferred_element_type=jnp.float32)

    def qkv_term(offset, amount):
        return jnp.einsum("jte,jde->td", grad_proj, w_qkv, preferred_element_type=jnp.float32)

    grad_normed = row_sums(qkv_term, own_rows)
    back0, gain0, bias0 = norm_backward(grad_normed, unit0, inv0, norm_gain[0])
    grad_inputs = (grad_middle + back0).astype(jnp.bfloat16)
    grad_qkv, grad_wout, grad_up, grad_down = lax.psum(
        (grad_qkv, grad_wout, grad_up, grad_down), "dp"
    )
    grad_gain, grad_bias = lax.psum(
        (
            jnp.stack([gain0, gain1, gain2, gain3], axis=0),
            jnp.stack([bias0, bias1, bias2, bias3], axis=0),
        ),
        ("dp", "tensor"),
    )
    return (output, grad_inputs, grad_qkv, grad_wout, grad_up, grad_down, grad_gain, grad_bias)


def solution(mesh):
    return jax.shard_map(
        per_device,
        mesh=mesh,
        in_specs=(
            P(("dp", "tensor"), None),
            P("dp", None),
            P(None, None, "tensor"),
            P("tensor", None),
            P(None, "tensor"),
            P("tensor", None),
            P(),
            P(),
            P(("dp", "tensor"), None),
        ),
        out_specs=(
            P(("dp", "tensor"), None),
            P(("dp", "tensor"), None),
            P(None, None, "tensor"),
            P("tensor", None),
            P(None, "tensor"),
            P("tensor", None),
            P(),
            P(),
        ),
        check_vma=False,
    )
```

profile of v0, /device:TPU:0, one launch (start us, length us, event | category | flops | bytes accessed | tf_op | source)
XLA Modules:
  0.0 931.0 jit_solution(6733210452404550416)
XLA Ops:
  7.2 1.3 convert_reduce_fusion.1
  11.7 2.1 fusion.106
  15.1 1.5 fusion.121
  17.7 21.6 %all-gather.5.cloned.1.call-done = bf16[1024,1024]{1,0:T(8,128)(2,1)} async-done(((bf16[256,1024]{1,0:T(8,128)(2,1)}), bf16[1024,1024]{1,0:T(8,128)(2,1)}) %all-gather.5.cloned.1.call-update) | async-done | bytes 2097168 | tf_op jit(solution)/shard_map/all_gather | solution.py:84
  39.3 3.9 fusion.90
  44.7 25.8 %while.27 = (s32[]{:T(128)}, bf16[2,512,4,64]{1,3,2,0:T(8,128)(2,1)}, f32[2,4,512]{2,1,0:T(4,128)S(1)}, s32[2]{0:T(128)S(1)}, s32[1,1024]{1,0:T(1,128)S(1)}, /*i...) while((s32[]{:T(128)}, ...), condition=%wide.region_7.8_spmd, body=%wide.region_4.7_spmd.sunk | while | flops 563739136 | bytes 33110264 | solution.py:118
  48.5 3.0 fusion.186
  51.4 2.3 fusion.187
  53.8 3.0 fusion.188
  61.4 3.0 fusion.186
  64.3 2.3 fusion.187
  66.7 3.0 fusion.188
  70.5 1.6 copy.24
  73.0 3.8 fusion.130
  76.8 44.7 %reduce-scatter.5.cloned.1.call-done = f32[256,1024]{1,0:T(8,128)} async-done(((f32[1024,1024]{1,0:T(8,128)}), f32[256,1024]{1,0:T(8,128)}) %reduce-scatter.5.cloned.1.call-update) | async-done | bytes 1048592 | tf_op jit(solution)/shard_map/reduce_scatter | solution.py:88
  121.5 1.4 reduce_sum.236
  122.9 1.5 multiply_reduce_fusion.7
  124.4 1.8 fusion.126
  128.7 22.2 %all-gather.7.cloned.1.call-done = bf16[1024,1024]{1,0:T(8,128)(2,1)} async-done(((bf16[256,1024]{1,0:T(8,128)(2,1)}), bf16[1024,1024]{1,0:T(8,128)(2,1)}) %all-gather.7.cloned.1.call-update) | async-done | bytes 2097168 | tf_op jit(solution)/shard_map/all_gather | solution.py:84
  150.9 5.8 multiply_convert_fusion.1
  156.8 1.3 copy-done.39
  158.1 4.4 fusion.131
  162.5 44.7 %reduce-scatter.7.cloned.1.call-done = f32[256,1024]{1,0:T(8,128)} async-done(((f32[1024,1024]{1,0:T(8,128)}), f32[256,1024]{1,0:T(8,128)}) %reduce-scatter.7.cloned.1.call-update) | async-done | bytes 1048592 | tf_op jit(solution)/shard_map/reduce_scatter | solution.py:88
  207.2 1.4 reduce_sum.240
  208.6 1.5 multiply_reduce_fusion.5
  210.0 1.9 fusion.118
  212.0 3.1 fusion.116
  215.2 22.7 %all-gather.9.cloned.1.call-done = bf16[1024,1024]{1,0:T(8,128)(2,1)} async-done(((bf16[256,1024]{1,0:T(8,128)(2,1)}), bf16[1024,1024]{1,0:T(8,128)(2,1)}) %all-gather.9.cloned.1.call-update) | async-done | bytes 2097168 | tf_op jit(solution)/shard_map/all_gather | solution.py:84
  237.9 6.2 fusion.85
  245.4 4.4 fusion.132
  249.9 44.7 %reduce-scatter.9.cloned.1.call-done = f32[256,1024]{1,0:T(8,128)} async-done(((f32[1024,1024]{1,0:T(8,128)}), f32[256,1024]{1,0:T(8,128)}) %reduce-scatter.9.cloned.1.call-update) | async-done | bytes 1048592 | tf_op jit(solution)/shard_map/reduce_scatter | solution.py:88
  294.6 1.7 multiply_reduce_fusion.1
  296.4 2.4 multiply_reduce_fusion.2
  300.9 22.6 %all-gather.11.cloned.1.call-done = bf16[1024,1024]{1,0:T(8,128)(2,1)} async-done(((bf16[256,1024]{1,0:T(8,128)(2,1)}), bf16[1024,1024]{1,0:T(8,128)(2,1)}) %all-gather.11.cloned.1.call-update) | async-done | bytes 2097168 | tf_op jit(solution)/shard_map/all_gather | solution.py:84
  323.6 2.4 convolution_convert_fusion
  326.0 130.7 %while.28 = (s32[]{:T(128)}, f32[1024,4,64]{0,2,1:T(8,128)}, f32[1024,4,64]{0,2,1:T(8,128)}, f32[2,512,4,64]{1,0,3,2:T(2,128)}, s32[2]{0:T(128)S(1)}, /*index=5*...) while((s32[]{:T(128)}, f32[1024,4,64]{0,2,1:T(8,128)}, ...), condition=%wide.region_25.26_spmd.clone, body=%wide.region_23.25_spmd.clone.sunk | while | flops 1399331328 | bytes 129562944 | solution.py:158
  330.0 1.4 fusion.200
  331.4 2.6 fusion.203
  335.6 4.6 fusion.199
  340.2 17.1 %fusion.204 = f32[1,512,4,64]{1,3,2,0:T(8,128)S(1)} fusion(bf16[1024,4,64]{0,2,1:T(8,128)(2,1)S(1)} %get-tuple-element.485, f32[4,512,1024]{2,1,0:T(8,128)} %fusion.199, f32[4,512,1024]{2,1,0:T(8,128)} %copy-done.2, f32[4,512]{1,0:T(4,128)S(1)} %dynamic-slice_bitcast_fusion.2, pred[512,1024]{1,0:T(8,128)(4,1)S(1)} %fusion.201), kind=kOutput, calls=%fused_computation.42.clone.1 | convolution fusion | flops 291507200 | bytes 18358272 | tf_op jit(solution)/shard_map/while/body/eval_jaxpr/hqk,khd->qhd/dot_general | solution.py:142
  357.4 23.1 %fusion.202 = f32[1024,4,64]{0,2,1:T(8,128)} fusion(f32[4,512,1024]{2,1,0:T(8,128)} %fusion.199, f32[4,512,1024]{2,1,0:T(8,128)} %copy-done.2, f32[4,512]{1,0:T(4,128)S(1)} %dynamic-slice_bitcast_fusion.2, pred[512,1024]{1,0:T(8,128)(4,1)S(1)} %fusion.201, f32[1024,4,64]{0,2,1:T(8,128)} %get-tuple-element.463, pred[]{:T(512)S(6)} %compare.3, ...), kind=kOutput, calls=%fused_computation.40.clone.1 | convolution fusion | flops 292031488 | bytes 36978692 | tf_op jit(solution)/shard_map/while/body/eval_jaxpr/hqk,qhd->khd/dot_general | solution.py:145
  381.0 10.3 %dynamic_update_slice.20 = f32[2,512,4,64]{1,0,3,2:T(2,128)} dynamic-update-slice(f32[2,512,4,64]{1,0,3,2:T(2,128)} %get-tuple-element.465, f32[1,512,4,64]{1,0,3,2:T(1,128)S(1)} %copy.61, s32[]{:T(128)S(6)} %copy.78, s32[]{:T(128)} %constant.76.clone.1..sunk.1, s32[]{:T(128)} %constant.76.clone.1..sunk.1, s32[]{:T(128)} %constant.76.clone.1..sunk.1) | dynamic-update-slice | bytes 1048580 | tf_op jit(solution)/shard_map/while/body/jit(dynamic_update_index_in_dim)/dynamic_update_slice | solution.py:158
  395.1 1.4 fusion.200
  396.6 2.6 fusion.203
  400.7 4.6 fusion.199
  405.3 17.1 %fusion.204 = f32[1,512,4,64]{1,3,2,0:T(8,128)S(1)} fusion(bf16[1024,4,64]{0,2,1:T(8,128)(2,1)S(1)} %get-tuple-element.485, f32[4,512,1024]{2,1,0:T(8,128)} %fusion.199, f32[4,512,1024]{2,1,0:T(8,128)} %copy-done.2, f32[4,512]{1,0:T(4,128)S(1)} %dynamic-slice_bitcast_fusion.2, pred[512,1024]{1,0:T(8,128)(4,1)S(1)} %fusion.201), kind=kOutput, calls=%fused_computation.42.clone.1 | convolution fusion | flops 291507200 | bytes 18358272 | tf_op jit(solution)/shard_map/while/body/eval_jaxpr/hqk,khd->qhd/dot_general | solution.py:142
  422.5 23.2 %fusion.202 = f32[1024,4,64]{0,2,1:T(8,128)} fusion(f32[4,512,1024]{2,1,0:T(8,128)} %fusion.199, f32[4,512,1024]{2,1,0:T(8,128)} %copy-done.2, f32[4,512]{1,0:T(4,128)S(1)} %dynamic-slice_bitcast_fusion.2, pred[512,1024]{1,0:T(8,128)(4,1)S(1)} %fusion.201, f32[1024,4,64]{0,2,1:T(8,128)} %get-tuple-element.463, pred[]{:T(512)S(6)} %compare.3, ...), kind=kOutput, calls=%fused_computation.40.clone.1 | convolution fusion | flops 292031488 | bytes 36978692 | tf_op jit(solution)/shard_map/while/body/eval_jaxpr/hqk,qhd->khd/dot_general | solution.py:145
  446.2 10.3 %dynamic_update_slice.20 = f32[2,512,4,64]{1,0,3,2:T(2,128)} dynamic-update-slice(f32[2,512,4,64]{1,0,3,2:T(2,128)} %get-tuple-element.465, f32[1,512,4,64]{1,0,3,2:T(1,128)S(1)} %copy.61, s32[]{:T(128)S(6)} %copy.78, s32[]{:T(128)} %constant.76.clone.1..sunk.1, s32[]{:T(128)} %constant.76.clone.1..sunk.1, s32[]{:T(128)} %constant.76.clone.1..sunk.1) | dynamic-update-slice | bytes 1048580 | tf_op jit(solution)/shard_map/while/body/jit(dynamic_update_index_in_dim)/dynamic_update_slice | solution.py:158
  456.7 2.1 reshape.326
  458.9 1.6 add_convert_fusion.3
  461.3 5.4 convolution_bitcast_fusion
  466.8 1.5 copy-done.38
  468.3 6.0 fusion.135
  474.4 4.4 fusion.134
  478.9 1.7 fusion.133
  480.6 3.5 fusion.93
  484.2 27.3 %reduce-scatter.11.cloned.1.call-done = f32[256,1024]{1,0:T(8,128)} async-done(((f32[1024,1024]{1,0:T(8,128)}), f32[256,1024]{1,0:T(8,128)}) %reduce-scatter.11.cloned.1.call-update) | async-done | bytes 1048592 | tf_op jit(solution)/shard_map/reduce_scatter | solution.py:88
  511.5 1.8 fusion.112
  513.3 43.8 %all-reduce = (f32[4,1024]{1,0:T(4,128)}, f32[4,1024]{1,0:T(4,128)}) all-reduce(f32[4,1024]{1,0:T(4,128)S(1)} %pad_maximum_fusion.7, f32[4,1024]{1,0:T(4,128)S(1)} %pad_maximum_fusion.8), channel_id=1, replica_groups=mesh['dp'=8,'tensor'=4] {'dp','tensor'}, use_global_device_ids=true, to_apply=%region_37.38 | all-reduce | flops 8192 | bytes 65536 | tf_op jit(solution)/shard_map/psum | solution.py:248
  557.1 2.4 fusion.111
  559.5 353.0 %all-reduce.4.cloned.1.call-done = (f32[3,1024,256]{1,2,0:T(8,128)}, f32[256,1024]{1,0:T(8,128)}, f32[1024,1024]{1,0:T(8,128)}, f32[1024,1024]{1,0:T(8,128)}) async-done(((f32[3,1024,256]{1,2,0:T(8,128)}, f32[256,1024]{1,0:T(8,128)}, f32[1024,1024]{1,0:T(8,128)}, f32[1024,1024]{1,0:T(8,128)}), (f32[3,1024,256]{1,2,0:T(8,128)}, f32[256,1024]{1,0:T(8,128)}, f32[1024,1024]{1,0:T(8,128)}, ...) | async-done | bytes 12582928 | tf_op jit(solution)/shard_map/psum | solution.py:245
  912.6 3.6 copy.30
  917.2 4.9 copy.91
  922.1 2.0 copy.92
  (182 shorter events, 29.0 us)
Async XLA Ops:
  7.2 143.8 %copy-start = (bf16[1024,1024]{1,0:T(8,128)(2,1)S(1)}, bf16[1024,1024]{1,0:T(8,128)(2,1)}, u32[]{:S(2)}) copy-start(bf16[1024,1024]{1,0:T(8,128)(2,1)} %param.17) | copy-start | bytes 6291460
  7.2 32.1 %all-gather.5.cloned.1.call-start = ((), (), s32[]{:S(2)}) async-start(), calls=%async_computation.4 | async-start | bytes 2621440 | tf_op jit(solution)/shard_map/all_gather | solution.py:84
  8.6 6.5 copy-start.31
  9.9 6.9 copy-start.33
  10.8 6.3 copy-start.29
  13.8 107.7 %reduce-scatter.5.cloned.1.call-start = ((), (), s32[]{:S(2)}) async-start(), calls=%async_computation.5 | async-start | bytes 5242880 | tf_op jit(solution)/shard_map/reduce_scatter | solution.py:88
  17.7 25.7 %copy-start.15 = (f32[1024,32]{0,1:T(8,128)}, f32[1024,32]{0,1:T(8,128)S(1)}, u32[]{:S(2)}) copy-start(f32[1024,32]{0,1:T(8,128)S(1)} %get-tuple-element.273) | copy-start | bytes 393220
  17.7 25.7 %copy-start.17 = (f32[1024,32]{0,1:T(8,128)}, f32[1024,32]{0,1:T(8,128)S(1)}, u32[]{:S(2)}) copy-start(f32[1024,32]{0,1:T(8,128)S(1)} %get-tuple-element.274) | copy-start | bytes 393220
  43.3 1.4 copy-start.14
  51.4 2.4 copy-start.23
  56.8 0.8 copy-start.24
  64.3 2.4 copy-start.23
  69.7 0.8 copy-start.24
  72.2 0.8 copy-start.10
  76.8 74.1 %all-gather.7.cloned.1.call-start = ((), (), s32[]{:S(2)}) async-start(), calls=%async_computation.6 | async-start | bytes 2621440 | tf_op jit(solution)/shard_map/all_gather | solution.py:84
  126.2 1.0 copy-start.3
  128.2 79.0 %reduce-scatter.7.cloned.1.call-start = ((), (), s32[]{:S(2)}) async-start(), calls=%async_computation.7 | async-start | bytes 5242880 | tf_op jit(solution)/shard_map/reduce_scatter | solution.py:88
  150.9 7.2 copy-start.35
  156.8 1.3 copy-start.39
  162.5 75.4 %all-gather.9.cloned.1.call-start = ((), (), s32[]{:S(2)}) async-start(), calls=%async_computation.8 | async-start | bytes 2621440 | tf_op jit(solution)/shard_map/all_gather | solution.py:84
  215.2 79.5 %reduce-scatter.9.cloned.1.call-start = ((), (), s32[]{:S(2)}) async-start(), calls=%async_computation.9 | async-start | bytes 5242880 | tf_op jit(solution)/shard_map/reduce_scatter | solution.py:88
  244.1 1.3 copy-start.40
  249.9 44.8 %copy-start.4 = (f32[256,1024]{1,0:T(8,128)S(1)}, f32[256,1024]{1,0:T(8,128)}, u32[]{:S(2)}) copy-start(f32[256,1024]{1,0:T(8,128)} %copy-done.3) | copy-start | bytes 3145732
  249.9 46.5 %copy-start.5 = (f32[256,1024]{1,0:T(8,128)S(1)}, f32[256,1024]{1,0:T(8,128)}, u32[]{:S(2)}) copy-start(f32[256,1024]{1,0:T(8,128)} %reduce-scatter.5.cloned.1.call-done) | copy-start | bytes 3145732
  249.9 73.7 %all-gather.11.cloned.1.call-start = ((), (), s32[]{:S(2)}) async-start(), calls=%async_computation.10 | async-start | bytes 2621440 | tf_op jit(solution)/shard_map/all_gather | solution.py:84
  298.7 1.0 copy-start.8
  299.7 26.3 %copy-start.6 = (bf16[1024,4,64]{0,2,1:T(8,128)(2,1)S(1)}, bf16[1024,4,64]{0,2,1:T(8,128)(2,1)}, u32[]{:S(2)}) copy-start(bf16[1024,4,64]{0,2,1:T(8,128)(2,1)} %get-tuple-element.521) | copy-start | bytes 1572868
  300.9 210.6 %reduce-scatter.11.cloned.1.call-start = ((), (), s32[]{:S(2)}) async-start(), calls=%async_computation.11 | async-start | bytes 5242880 | tf_op jit(solution)/shard_map/reduce_scatter | solution.py:88
  326.0 132.8 %copy-start.16 = (f32[1024,32]{0,1:T(8,128)S(1)}, f32[1024,32]{0,1:T(8,128)}, u32[]{:S(2)}) copy-start(f32[1024,32]{0,1:T(8,128)} %copy-done.15) | copy-start | bytes 393220
  326.0 132.8 %copy-start.18 = (f32[1024,32]{0,1:T(8,128)S(1)}, f32[1024,32]{0,1:T(8,128)}, u32[]{:S(2)}) copy-start(f32[1024,32]{0,1:T(8,128)} %copy-done.17) | copy-start | bytes 393220
  330.0 1.4 copy-start.19
  331.4 3.2 copy-start.2
  334.6 1.0 copy-start.20
  395.1 1.4 copy-start.19
  396.5 3.2 copy-start.2
  399.8 1.0 copy-start.20
  458.8 2.1 copy-start.21
  461.0 5.8 copy-start.25
  461.3 5.5 copy-start.27
  466.7 1.6 copy-start.38
  466.8 445.8 %all-reduce.4.cloned.1.call-start = ((), (), s32[]{:S(2)}) async-start(), calls=%async_computation.12 | async-start | bytes 25165824 | tf_op jit(solution)/shard_map/psum | solution.py:245
  468.3 6.1 copy-start.37
  468.3 6.1 copy-start.41
  474.4 4.5 copy-start.11
  474.4 4.5 copy-start.13
  474.4 6.2 copy-start.26
  474.4 6.2 copy-start.28
  474.4 6.2 copy-start.36
  484.1 27.4 %copy-start.7 = (bf16[256,1024]{1,0:T(8,128)(2,1)S(1)}, bf16[256,1024]{1,0:T(8,128)(2,1)}, u32[]{:S(2)}) copy-start(bf16[256,1024]{1,0:T(8,128)(2,1)} %param.13) | copy-start | bytes 1572868
  484.1 27.4 %copy-start.30 = (f32[1,1024]{1,0:T(1,128)S(1)}, f32[1,1024]{1,0:T(1,128)}, u32[]{:S(2)}) copy-start(f32[1,1024]{1,0:T(1,128)} %copy-done.29) | copy-start | bytes 12292
  484.1 27.4 %copy-start.32 = (f32[256]{0:T(256)S(1)}, f32[256]{0:T(256)}, u32[]{:S(2)}) copy-start(f32[256]{0:T(256)} %copy-done.31) | copy-start | bytes 3076
  484.1 27.4 %copy-start.34 = (f32[256]{0:T(256)S(1)}, f32[256]{0:T(256)}, u32[]{:S(2)}) copy-start(f32[256]{0:T(256)} %copy-done.33) | copy-start | bytes 3076
  484.1 73.0 %copy-start.9 = (f32[256,1024]{1,0:T(8,128)S(1)}, f32[256,1024]{1,0:T(8,128)}, u32[]{:S(2)}) copy-start(f32[256,1024]{1,0:T(8,128)} %copy-done.8) | copy-start | bytes 3145732
  912.6 3.6 copy-start.22
  917.2 4.9 copy-start.12
  917.2 7.0 copy-start.1
Sparse Core Ops, SparseCore 0:
  14.0 25.2 all-gather.4
  76.9 44.5 reduce-scatter.4
  128.3 22.5 all-gather.6
  162.6 44.5 reduce-scatter.6
  215.3 22.5 all-gather.8
  250.0 44.5 reduce-scatter.8
  301.0 22.5 all-gather.10
  466.9 44.5 reduce-scatter.10
  516.8 395.6 all-reduce.3
where the time goes:
time: 941 us; the launch traced here: 931 us
  waiting for transfers between devices  604 us (64%)
  matrix products  162 us (17%)
  local copies, waits for them, and re-layouts  55 us (6%)
  blocking collectives  43.8 us (5%)
  other arithmetic  42.7 us (5%)
  between operations  14.8 us (2%)
    psum x1, waiting for transfers between devices, per_device(): lax.psum((grad_qkv, grad_wout, grad_up, grad_down), 'dp')  353 us
    reduce_scatter x4, waiting for transfers between devices, row_sums(): lax.psum_scatter(term(jnp.int32(0), own_rows * lax.axis_size('tensor')),...  161 us
    all_gather x4, waiting for transfers between devices, gather_rows(): return lax.all_gather(values_in, 'tensor', axis=0, tiled=True)  89.1 us
    dot_general x2, matrix products, step_back(): jnp.einsum('hqk,qhd->khd', grad_scores, query_block, preferred_element_ty...  46.3 us
    psum x1, blocking collectives, per_device(): lax.psum((jnp.stack([gain0, gain1, gain2, gain3], axis=0), jnp.stack([bia...  43.8 us
    dot_general x2, matrix products, step_back(): jnp.einsum('hqk,khd->qhd', grad_scores, key_rot, preferred_element_type=j...  34.3 us
    dynamic_update_slice x4, local copies, waits for them, and re-layouts, attention_backward(): lax.scan(step_back, (zeros_kv, zeros_kv), (offsets, log_total))  21.7 us
  transfers between devices with their start and end apart: 9, of which 9 were waited for; matrix products, arithmetic and copies ran while one was open for 3% of the time, Pallas kernels for 0%

commit v1 on v0

--- a/solution.py
+++ b/solution.py
@@ -5,6 +5,28 @@
 
 HEAD_DIM = 64
 eps = 1e-05
+
+
+def joined_along(blocks, dim):
+    blocks = jnp.moveaxis(blocks, 0, dim)
+    shape = blocks.shape
+    return blocks.reshape(*shape[:dim], shape[dim] * shape[dim + 1], *shape[dim + 2 :])
+
+
+def collected_by_bits(value, axis):
+    peers = lax.axis_size(axis)
+    tiles = value[None]
+    for level in range(peers.bit_length() - 1):
+        distance = 1 << level
+        received = lax.ppermute(tiles, axis, [(i, i ^ distance) for i in range(peers)])
+        both = jnp.stack([tiles, received])
+        upper = lax.axis_index(axis) >> level & 1
+        tiles = jnp.where(upper == 0, both, both[::-1]).reshape(-1, *value.shape)
+    return tiles
+
+
+def doubled_up(shard, axis, dim):
+    return joined_along(collected_by_bits(shard, axis), dim)
 
 
 def rope_tables(doc_row):
@@ -81,7 +103,7 @@
 
 
 def gather_rows(values_in):
-    return lax.all_gather(values_in, "tensor", axis=0, tiled=True)
+    return doubled_up(values_in, "tensor", 0)
 
 
 def row_sums(term, own_rows):

time: 941 us -> 973 us (1.034)
  waiting for transfers between devices: 604 us -> 618 us
    ppermute x0 -> x8, waiting for transfers between devices: none -> 102 us  [collected_by_bits(): lax.ppermute(tiles, axis, [(i, i ^ distance) for i in range(peers)])]
    all_gather x4 -> x0, waiting for transfers between devices: 89.1 us -> none  [gather_rows(): return lax.all_gather(values_in, 'tensor', axis=0, tiled=True)]
    unnamed x79 -> x99, local copies, waits for them, and re-layouts: 18.3 us -> 22.5 us
  transfers between devices with their start and end apart: 9 -> 13, of which waited for: 9 -> 13; matrix products, arithmetic and copies ran while one was open for 3% -> 2% of each run, Pallas kernels for 0% -> 0%
where the time goes in v1:
time: 973 us; the launch traced here: 963 us
  waiting for transfers between devices  618 us (64%)
  matrix products  154 us (16%)
  local copies, waits for them, and re-layouts  58.9 us (6%)
  other arithmetic  50.7 us (5%)
  blocking collectives  43.6 us (4%)
  loops' own time  17.9 us (2%)
  between operations  14.9 us (2%)
    psum x1, waiting for transfers between devices, per_device(): lax.psum((grad_qkv, grad_wout, grad_up, grad_down), 'dp')  353 us
    reduce_scatter x4, waiting for transfers between devices, row_sums(): lax.psum_scatter(term(jnp.int32(0), own_rows * lax.axis_size('tensor')),...  163 us
    ppermute x8, waiting for transfers between devices, collected_by_bits(): lax.ppermute(tiles, axis, [(i, i ^ distance) for i in range(peers)])  102 us
    dot_general x2, matrix products, step_back(): jnp.einsum('hqk,qhd->khd', grad_scores, query_block, preferred_element_ty...  46.3 us
    psum x1, blocking collectives, per_device(): lax.psum((jnp.stack([gain0, gain1, gain2, gain3], axis=0), jnp.stack([bia...  43.6 us
    dot_general x2, matrix products, step_back(): jnp.einsum('hqk,khd->qhd', grad_scores, key_rot, preferred_element_type=j...  34.3 us
    unnamed x99, local copies, waits for them, and re-layouts  22.5 us
    dynamic_update_slice x4, local copies, waits for them, and re-layouts, attention_backward(): lax.scan(step_back, (zeros_kv, zeros_kv), (offsets, log_total))  21.7 us
  transfers between devices with their start and end apart: 13, of which 13 were waited for; matrix products, arithmetic and copies ran while one was open for 2% of the time, Pallas kernels for 0%

profile of v1, /device:TPU:0, one launch (start us, length us, event | category | flops | bytes accessed | tf_op | source)
XLA Modules:
  0.0 963.1 jit_solution(10013970504653819965)
XLA Ops:
  13.6 1.7 collective-permute-done
  16.4 1.7 fusion.110
  18.1 2.8 collective-permute-start.1
  23.4 21.4 %collective-permute-done.1 = bf16[2,256,1024]{2,1,0:T(8,128)(2,1)} collective-permute-done((bf16[2,256,1024]{2,1,0:T(8,128)(2,1)}, bf16[2,256,1024]{2,1,0:T(8,128)(2,1)}, u32[]{:S(2)}, u32[]{:S(2)}) %collective-permute-start.1) | collective-permute-done | bytes 1048608 | tf_op jit(solution)/shard_map/ppermute | solution.py:21
  44.8 1.9 pad_maximum_fusion
  47.2 1.9 convolution_bitcast_fusion.2
  50.6 25.8 %while.27 = (s32[]{:T(128)}, bf16[2,512,4,64]{1,3,2,0:T(8,128)(2,1)}, f32[2,4,512]{2,1,0:T(4,128)S(1)}, s32[2]{0:T(128)S(1)}, s32[1,1024]{1,0:T(1,128)S(1)}, /*i...) while((s32[]{:T(128)}, ...), condition=%wide.region_7.8_spmd, body=%wide.region_4.7_spmd.sunk | while | flops 563739136 | bytes 33110264 | solution.py:140
  54.3 3.0 fusion.192
  57.3 2.3 fusion.193
  59.7 3.0 fusion.194
  67.3 3.0 fusion.192
  70.2 2.3 fusion.193
  72.6 3.0 fusion.194
  76.4 1.6 copy.26
  78.9 3.8 fusion.130
  83.0 45.9 %reduce-scatter.5.cloned.1.call-done = f32[256,1024]{1,0:T(8,128)} async-done(((f32[1024,1024]{1,0:T(8,128)}), f32[256,1024]{1,0:T(8,128)}) %reduce-scatter.5.cloned.1.call-update) | async-done | bytes 1048592 | tf_op jit(solution)/shard_map/reduce_scatter | solution.py:110
  130.3 1.5 multiply_reduce_fusion.7
  131.8 1.8 fusion.126
  136.8 24.9 %collective-permute-done.3 = bf16[2,256,1024]{2,1,0:T(8,128)(2,1)S(1)} collective-permute-done((bf16[2,256,1024]{2,1,0:T(8,128)(2,1)S(1)}, bf16[2,256,1024]{2,1,0:T(8,128)(2,1)S(1)}, u32[]{:S(2)}, u32[]{:S(2)}) %collective-permute-start.3) | collective-permute-done | bytes 1048608 | tf_op jit(solution)/shard_map/ppermute | solution.py:21
  162.5 4.1 multiply_convert_fusion.1
  167.9 4.3 fusion.131
  172.4 44.7 %reduce-scatter.7.cloned.1.call-done = f32[256,1024]{1,0:T(8,128)} async-done(((f32[1024,1024]{1,0:T(8,128)}), f32[256,1024]{1,0:T(8,128)}) %reduce-scatter.7.cloned.1.call-update) | async-done | bytes 1048592 | tf_op jit(solution)/shard_map/reduce_scatter | solution.py:110
  218.4 1.5 multiply_reduce_fusion.5
  219.9 2.5 fusion.108
  222.4 3.0 fusion.106
  225.4 1.9 collective-permute-done.4
  228.1 24.9 %collective-permute-done.5 = bf16[2,256,1024]{2,1,0:T(8,128)(2,1)S(1)} collective-permute-done((bf16[2,256,1024]{2,1,0:T(8,128)(2,1)S(1)}, bf16[2,256,1024]{2,1,0:T(8,128)(2,1)S(1)}, u32[]{:S(2)}, u32[]{:S(2)}) %collective-permute-start.5) | collective-permute-done | bytes 1048608 | tf_op jit(solution)/shard_map/ppermute | solution.py:21
  254.5 2.0 copy-done.48
  256.5 3.6 fusion.85
  261.5 4.5 fusion.132
  266.0 44.7 %reduce-scatter.9.cloned.1.call-done = f32[256,1024]{1,0:T(8,128)} async-done(((f32[1024,1024]{1,0:T(8,128)}), f32[256,1024]{1,0:T(8,128)}) %reduce-scatter.9.cloned.1.call-update) | async-done | bytes 1048592 | tf_op jit(solution)/shard_map/reduce_scatter | solution.py:110
  310.7 1.7 multiply_reduce_fusion.1
  312.4 2.4 multiply_reduce_fusion.2
  315.6 1.5 collective-permute-done.6
  318.1 25.0 %collective-permute-done.7 = bf16[2,256,1024]{2,1,0:T(8,128)(2,1)} collective-permute-done((bf16[2,256,1024]{2,1,0:T(8,128)(2,1)S(1)}, bf16[2,256,1024]{2,1,0:T(8,128)(2,1)}, u32[]{:S(2)}, u32[]{:S(2)}) %collective-permute-start.7) | collective-permute-done | bytes 1048608 | tf_op jit(solution)/shard_map/ppermute | solution.py:21
  343.0 1.5 pad_maximum_fusion.3
  347.2 140.6 %while.28 = (s32[]{:T(128)}, f32[1024,4,64]{0,2,1:T(8,128)}, f32[1024,4,64]{0,2,1:T(8,128)}, f32[2,512,4,64]{1,0,3,2:T(2,128)}, s32[2]{0:T(128)S(1)}, /*index=5*...) while((s32[]{:T(128)}, f32[1024,4,64]{0,2,1:T(8,128)}, ...), condition=%wide.region_25.26_spmd.clone, body=%wide.region_23.25_spmd.clone.sunk | while | flops 1399331328 | bytes 129562944 | solution.py:180
  360.7 1.4 fusion.206
  362.2 2.6 fusion.209
  366.4 4.6 fusion.205
  371.0 17.1 %fusion.210 = f32[1,512,4,64]{1,3,2,0:T(8,128)S(1)} fusion(bf16[1024,4,64]{0,2,1:T(8,128)(2,1)S(1)} %get-tuple-element.495, f32[4,512,1024]{2,1,0:T(8,128)} %fusion.205, f32[4,512,1024]{2,1,0:T(8,128)} %copy-done.2, f32[4,512]{1,0:T(4,128)S(1)} %dynamic-slice_bitcast_fusion.2, pred[512,1024]{1,0:T(8,128)(4,1)S(1)} %fusion.207), kind=kOutput, calls=%fused_computation.42.clone.1 | convolution fusion | flops 291507200 | bytes 18358272 | tf_op jit(solution)/shard_map/while/body/eval_jaxpr/hqk,khd->qhd/dot_general | solution.py:164
  388.2 23.1 %fusion.208 = f32[1024,4,64]{0,2,1:T(8,128)} fusion(f32[4,512,1024]{2,1,0:T(8,128)} %fusion.205, f32[4,512,1024]{2,1,0:T(8,128)} %copy-done.2, f32[4,512]{1,0:T(4,128)S(1)} %dynamic-slice_bitcast_fusion.2, pred[512,1024]{1,0:T(8,128)(4,1)S(1)} %fusion.207, f32[1024,4,64]{0,2,1:T(8,128)} %get-tuple-element.473, pred[]{:T(512)S(6)} %compare.3, ...), kind=kOutput, calls=%fused_computation.40.clone.1 | convolution fusion | flops 292031488 | bytes 36978692 | tf_op jit(solution)/shard_map/while/body/eval_jaxpr/hqk,qhd->khd/dot_general | solution.py:167
  411.9 10.3 %dynamic_update_slice.20 = f32[2,512,4,64]{1,0,3,2:T(2,128)} dynamic-update-slice(f32[2,512,4,64]{1,0,3,2:T(2,128)} %get-tuple-element.475, f32[1,512,4,64]{1,0,3,2:T(1,128)S(1)} %copy.65, s32[]{:T(128)S(6)} %copy.82, s32[]{:T(128)} %constant.80.clone.1..sunk.1, s32[]{:T(128)} %constant.80.clone.1..sunk.1, s32[]{:T(128)} %constant.80.clone.1..sunk.1) | dynamic-update-slice | bytes 1048580 | tf_op jit(solution)/shard_map/while/body/jit(dynamic_update_index_in_dim)/dynamic_update_slice | solution.py:180
  427.6 2.6 fusion.209
  431.9 4.6 fusion.205
  436.5 17.1 %fusion.210 = f32[1,512,4,64]{1,3,2,0:T(8,128)S(1)} fusion(bf16[1024,4,64]{0,2,1:T(8,128)(2,1)S(1)} %get-tuple-element.495, f32[4,512,1024]{2,1,0:T(8,128)} %fusion.205, f32[4,512,1024]{2,1,0:T(8,128)} %copy-done.2, f32[4,512]{1,0:T(4,128)S(1)} %dynamic-slice_bitcast_fusion.2, pred[512,1024]{1,0:T(8,128)(4,1)S(1)} %fusion.207), kind=kOutput, calls=%fused_computation.42.clone.1 | convolution fusion | flops 291507200 | bytes 18358272 | tf_op jit(solution)/shard_map/while/body/eval_jaxpr/hqk,khd->qhd/dot_general | solution.py:164
  453.6 23.2 %fusion.208 = f32[1024,4,64]{0,2,1:T(8,128)} fusion(f32[4,512,1024]{2,1,0:T(8,128)} %fusion.205, f32[4,512,1024]{2,1,0:T(8,128)} %copy-done.2, f32[4,512]{1,0:T(4,128)S(1)} %dynamic-slice_bitcast_fusion.2, pred[512,1024]{1,0:T(8,128)(4,1)S(1)} %fusion.207, f32[1024,4,64]{0,2,1:T(8,128)} %get-tuple-element.473, pred[]{:T(512)S(6)} %compare.3, ...), kind=kOutput, calls=%fused_computation.40.clone.1 | convolution fusion | flops 292031488 | bytes 36978692 | tf_op jit(solution)/shard_map/while/body/eval_jaxpr/hqk,qhd->khd/dot_general | solution.py:167
  477.3 10.3 %dynamic_update_slice.20 = f32[2,512,4,64]{1,0,3,2:T(2,128)} dynamic-update-slice(f32[2,512,4,64]{1,0,3,2:T(2,128)} %get-tuple-element.475, f32[1,512,4,64]{1,0,3,2:T(1,128)S(1)} %copy.65, s32[]{:T(128)S(6)} %copy.82, s32[]{:T(128)} %constant.80.clone.1..sunk.1, s32[]{:T(128)} %constant.80.clone.1..sunk.1, s32[]{:T(128)} %constant.80.clone.1..sunk.1) | dynamic-update-slice | bytes 1048580 | tf_op jit(solution)/shard_map/while/body/jit(dynamic_update_index_in_dim)/dynamic_update_slice | solution.py:180
  487.9 2.1 reshape.342
  490.0 1.6 add_convert_fusion.3
  493.7 5.2 convolution_bitcast_fusion
  499.0 1.5 copy-done.20
  500.5 6.1 fusion.135
  506.6 4.4 fusion.134
  511.1 1.7 fusion.133
  512.8 3.5 convolution_bitcast_fusion.1
  516.4 27.3 %reduce-scatter.11.cloned.1.call-done = f32[256,1024]{1,0:T(8,128)} async-done(((f32[1024,1024]{1,0:T(8,128)}), f32[256,1024]{1,0:T(8,128)}) %reduce-scatter.11.cloned.1.call-update) | async-done | bytes 1048592 | tf_op jit(solution)/shard_map/reduce_scatter | solution.py:110
  543.7 1.8 fusion.102
  545.6 43.6 %all-reduce = (f32[4,1024]{1,0:T(4,128)}, f32[4,1024]{1,0:T(4,128)}) all-reduce(f32[4,1024]{1,0:T(4,128)S(1)} %pad_maximum_fusion.15, f32[4,1024]{1,0:T(4,128)S(1)} %pad_maximum_fusion.16), channel_id=1, replica_groups=mesh['dp'=8,'tensor'=4] {'dp','tensor'}, use_global_device_ids=true, to_apply=%region_37.38 | all-reduce | flops 8192 | bytes 65536 | tf_op jit(solution)/shard_map/psum | solution.py:270
  589.2 2.4 fusion.101
  591.6 353.0 %all-reduce.4.cloned.1.call-done = (f32[3,1024,256]{1,2,0:T(8,128)}, f32[256,1024]{1,0:T(8,128)}, f32[1024,1024]{1,0:T(8,128)}, f32[1024,1024]{1,0:T(8,128)}) async-done(((f32[3,1024,256]{1,2,0:T(8,128)}, f32[256,1024]{1,0:T(8,128)}, f32[1024,1024]{1,0:T(8,128)}, f32[1024,1024]{1,0:T(8,128)}), (f32[3,1024,256]{1,2,0:T(8,128)}, f32[256,1024]{1,0:T(8,128)}, f32[1024,1024]{1,0:T(8,128)}, ...) | async-done | bytes 12582928 | tf_op jit(solution)/shard_map/psum | solution.py:267
  944.6 3.6 copy.34
  949.2 4.9 copy.95
  954.1 2.0 copy.96
  (224 shorter events, 47.3 us)
Async XLA Ops:
  7.2 155.3 %copy-start = (bf16[1024,1024]{1,0:T(8,128)(2,1)S(1)}, bf16[1024,1024]{1,0:T(8,128)(2,1)}, u32[]{:S(2)}) copy-start(bf16[1024,1024]{1,0:T(8,128)(2,1)} %param.17) | copy-start | bytes 6291460
  7.2 13.8 %copy-start.21 = (s32[1,1024]{1,0:T(1,128)S(1)}, s32[1,1024]{1,0:T(1,128)}, u32[]{:S(2)}) copy-start(s32[1,1024]{1,0:T(1,128)} %param.14) | copy-start | bytes 12292
  7.2 121.7 %reduce-scatter.5.cloned.1.call-start = ((), (), s32[]{:S(2)}) async-start(), calls=%async_computation.4 | async-start | bytes 5242880 | tf_op jit(solution)/shard_map/reduce_scatter | solution.py:110
  8.6 12.9 %copy-start.39 = (f32[256]{0:T(256)}, f32[256]{0:T(256)S(1)}, u32[]{:S(2)}) copy-start(f32[256]{0:T(256)S(1)} %broadcast_multiply_fusion.11) | copy-start | bytes 3076
  9.9 36.7 %copy-start.41 = (f32[256]{0:T(256)}, f32[256]{0:T(256)S(1)}, u32[]{:S(2)}) copy-start(f32[256]{0:T(256)S(1)} %add_rsqrt_fusion.3) | copy-start | bytes 3076
  10.8 2.8 copy-start.37
  13.0 2.2 collective-permute-start
  18.1 26.6 %collective-permute-start.1 = (bf16[2,256,1024]{2,1,0:T(8,128)(2,1)}, bf16[2,256,1024]{2,1,0:T(8,128)(2,1)}, u32[]{:S(2)}, u32[]{:S(2)}) collective-permute-start(bf16[2,256,1024]{2,1,0:T(8,128)(2,1)} %get-tuple-element.268), channel_id=1, source_target_pairs={{0,2},{1,3},{2,0},{3,1},{4,6},{5,7},{6,4},{7,5},{8,10},{9,11},{10,... | collective-permute-start | bytes 3145736 | tf_op jit(solution)/shard_map/ppermute | solution.py:21
  23.4 26.0 %copy-start.22 = (f32[1024,32]{0,1:T(8,128)}, f32[1024,32]{0,1:T(8,128)S(1)}, u32[]{:S(2)}) copy-start(f32[1024,32]{0,1:T(8,128)S(1)} %get-tuple-element.283) | copy-start | bytes 393220
  23.4 26.0 %copy-start.24 = (f32[1024,32]{0,1:T(8,128)}, f32[1024,32]{0,1:T(8,128)S(1)}, u32[]{:S(2)}) copy-start(f32[1024,32]{0,1:T(8,128)S(1)} %get-tuple-element.284) | copy-start | bytes 393220
  44.8 2.5 copy-start.47
  47.2 1.9 copy-start.15
  57.3 2.4 copy-start.31
  70.2 2.4 copy-start.31
  82.7 134.3 %reduce-scatter.7.cloned.1.call-start = ((), (), s32[]{:S(2)}) async-start(), calls=%async_computation.5 | async-start | bytes 5242880 | tf_op jit(solution)/shard_map/reduce_scatter | solution.py:110
  134.1 2.0 collective-permute-start.2
  136.4 25.3 %collective-permute-start.3 = (bf16[2,256,1024]{2,1,0:T(8,128)(2,1)S(1)}, bf16[2,256,1024]{2,1,0:T(8,128)(2,1)S(1)}, u32[]{:S(2)}, u32[]{:S(2)}) collective-permute-start(bf16[2,256,1024]{2,1,0:T(8,128)(2,1)S(1)} %get-tuple-element.266), channel_id=1, source_target_pairs={{0,2},{1,3},{2,0},{3,1},{4,6},{5,7},{6,4},{7,5},{8,10},{9,11},{10,... | collective-permute-start | bytes 3145736 | tf_op jit(solution)/shard_map/ppermute | solution.py:21
  162.5 4.1 copy-start.17
  162.5 5.4 copy-start.45
  166.6 1.3 copy-start.49
  172.3 138.4 %reduce-scatter.9.cloned.1.call-start = ((), (), s32[]{:S(2)}) async-start(), calls=%async_computation.6 | async-start | bytes 5242880 | tf_op jit(solution)/shard_map/reduce_scatter | solution.py:110
  225.4 1.9 collective-permute-start.4
  227.6 25.3 %collective-permute-start.5 = (bf16[2,256,1024]{2,1,0:T(8,128)(2,1)S(1)}, bf16[2,256,1024]{2,1,0:T(8,128)(2,1)S(1)}, u32[]{:S(2)}, u32[]{:S(2)}) collective-permute-start(bf16[2,256,1024]{2,1,0:T(8,128)(2,1)S(1)} %get-tuple-element.264), channel_id=1, source_target_pairs={{0,2},{1,3},{2,0},{3,1},{4,6},{5,7},{6,4},{7,5},{8,10},{9,11},{10,... | collective-permute-start | bytes 3145736 | tf_op jit(solution)/shard_map/ppermute | solution.py:21
  252.9 1.6 copy-start.46
  252.9 3.6 copy-start.48
  253.7 6.4 copy-start.19
  260.1 1.3 copy-start.50
  265.9 44.8 %copy-start.4 = (f32[256,1024]{1,0:T(8,128)S(1)}, f32[256,1024]{1,0:T(8,128)}, u32[]{:S(2)}) copy-start(f32[256,1024]{1,0:T(8,128)} %copy-done.3) | copy-start | bytes 3145732
  265.9 46.5 %copy-start.5 = (f32[256,1024]{1,0:T(8,128)S(1)}, f32[256,1024]{1,0:T(8,128)}, u32[]{:S(2)}) copy-start(f32[256,1024]{1,0:T(8,128)} %reduce-scatter.5.cloned.1.call-done) | copy-start | bytes 3145732
  265.9 277.8 %reduce-scatter.11.cloned.1.call-start = ((), (), s32[]{:S(2)}) async-start(), calls=%async_computation.7 | async-start | bytes 5242880 | tf_op jit(solution)/shard_map/reduce_scatter | solution.py:110
  314.8 2.9 copy-start.8
  315.2 2.0 collective-permute-start.6
  317.6 25.4 %collective-permute-start.7 = (bf16[2,256,1024]{2,1,0:T(8,128)(2,1)S(1)}, bf16[2,256,1024]{2,1,0:T(8,128)(2,1)}, u32[]{:S(2)}, u32[]{:S(2)}) collective-permute-start(bf16[2,256,1024]{2,1,0:T(8,128)(2,1)S(1)} %get-tuple-element.262), channel_id=1, source_target_pairs={{0,2},{1,3},{2,0},{3,1},{4,6},{5,7},{6,4},{7,5},{8,10},{9,11},{10,... | collective-permute-start | bytes 3145736 | tf_op jit(solution)/shard_map/ppermute | solution.py:21
  343.0 3.4 copy-start.30
  344.5 2.7 copy-start.6
  345.1 1.3 copy-start.10
  347.2 142.8 %copy-start.23 = (f32[1024,32]{0,1:T(8,128)S(1)}, f32[1024,32]{0,1:T(8,128)}, u32[]{:S(2)}) copy-start(f32[1024,32]{0,1:T(8,128)} %copy-done.22) | copy-start | bytes 393220
  347.2 142.8 %copy-start.25 = (f32[1024,32]{0,1:T(8,128)S(1)}, f32[1024,32]{0,1:T(8,128)}, u32[]{:S(2)}) copy-start(f32[1024,32]{0,1:T(8,128)} %copy-done.24) | copy-start | bytes 393220
  360.7 1.4 copy-start.26
  362.1 3.2 copy-start.2
  365.4 1.1 copy-start.27
  426.2 1.4 copy-start.26
  427.6 3.2 copy-start.2
  430.8 1.1 copy-start.27
  490.0 2.1 copy-start.28
  498.9 1.6 copy-start.20
  499.0 445.6 %all-reduce.4.cloned.1.call-start = ((), (), s32[]{:S(2)}) async-start(), calls=%async_computation.8 | async-start | bytes 25165824 | tf_op jit(solution)/shard_map/psum | solution.py:267
  500.5 6.1 copy-start.18
  500.5 6.1 copy-start.51
  506.6 4.5 copy-start.11
  506.6 4.5 copy-start.13
  506.6 6.2 copy-start.16
  506.6 6.2 copy-start.34
  506.6 6.2 copy-start.36
  516.3 27.4 %copy-start.7 = (bf16[256,1024]{1,0:T(8,128)(2,1)S(1)}, bf16[256,1024]{1,0:T(8,128)(2,1)}, u32[]{:S(2)}) copy-start(bf16[256,1024]{1,0:T(8,128)(2,1)} %param.13) | copy-start | bytes 1572868
  516.3 27.4 %copy-start.38 = (f32[1,1024]{1,0:T(1,128)S(1)}, f32[1,1024]{1,0:T(1,128)}, u32[]{:S(2)}) copy-start(f32[1,1024]{1,0:T(1,128)} %copy-done.37) | copy-start | bytes 12292
  516.3 27.4 %copy-start.40 = (f32[256]{0:T(256)S(1)}, f32[256]{0:T(256)}, u32[]{:S(2)}) copy-start(f32[256]{0:T(256)} %copy-done.39) | copy-start | bytes 3076
  516.3 27.4 %copy-start.42 = (f32[256]{0:T(256)S(1)}, f32[256]{0:T(256)}, u32[]{:S(2)}) copy-start(f32[256]{0:T(256)} %copy-done.41) | copy-start | bytes 3076
  516.3 29.2 %copy-start.44 = (f32[1024]{0:T(1024)S(1)}, f32[1024]{0:T(1024)}, u32[]{:S(2)}) copy-start(f32[1024]{0:T(1024)} %get-tuple-element.186) | copy-start | bytes 12292
  516.4 29.2 %copy-start.43 = (f32[1024]{0:T(1024)S(1)}, f32[1024]{0:T(1024)}, u32[]{:S(2)}) copy-start(f32[1024]{0:T(1024)} %get-tuple-element.195) | copy-start | bytes 12292
  516.4 72.8 %copy-start.9 = (f32[256,1024]{1,0:T(8,128)S(1)}, f32[256,1024]{1,0:T(8,128)}, u32[]{:S(2)}) copy-start(f32[256,1024]{1,0:T(8,128)} %copy-done.8) | copy-start | bytes 3145732
  944.6 3.6 copy-start.29
  949.2 4.9 copy-start.14
  949.2 7.0 copy-start.1
  (6 other events, 5.0 us)
Sparse Core Ops, SparseCore 0:
  82.8 46.0 reduce-scatter.4
  172.4 44.5 reduce-scatter.6
  266.1 44.5 reduce-scatter.8
  499.1 44.5 reduce-scatter.10
  548.9 395.6 all-reduce.3
